TPU v7x, 128 devices: a whole 4x4x4 slice. The times are simulated.
128 devices in a mesh: layer: 4 (over y_lo, core), latent: 16 (over x, z), row: 2 (over y_hi).
Axes of the slice: x: 4, y: 4 (y_hi: 2, y_lo: 2; y = y_hi * 2 + y_lo), z: 4, core: 2. Of those that a mesh axis runs over, the one named last changes fastest.
Arguments:
- inputs: bfloat16 [1024, 4, 3584], P('row', 'layer'), may hold values from -6 to 6
- clean_acts: bfloat16 [1024, 4, 3584], P('row', 'layer'), may hold values from -6 to 6
- enc_weight: bfloat16 [4, 3584, 12288], P('layer', None, 'latent'), may hold values from -0.0625 to 0.0625
- enc_bias: float32 [12288], P('latent'), may hold values from -3 to 3
- dec_weight: bfloat16 [4, 12288, 3584], P('layer', 'latent'), may hold values from -0.109375 to 0.109375
- dec_bias: float32 [4, 3584], P('layer'), may hold values from -3 to 3
- pairing: int32 [1024], replicated, may hold values from 0 to 1023, each once
- targets: int32 [1024], replicated, may hold values from 0 to 12287
Outputs:
- input_grad: bfloat16 [1024, 4, 3584], P('row', 'layer', 'latent')
Inputs may be any that keep to these rules, and one draw needn't show every extreme that they name: pairing is a permutation of the rows.
All inputs are finite; a program needn't handle non-finite values.
Results may differ from a plain program's by a relative error of at most 0.018.
Values may be sent and summed in bfloat16 or wider, within the bound.
A program may use at most 128 MiB of HBM per device.

v0:
```python
import jax
import jax.numpy as jnp
from jax import lax
from jax.sharding import PartitionSpec as P

MARGIN = 16.0


def local(inputs, clean_acts, enc_weight, enc_bias, dec_weight, dec_bias, pairing, targets):
    row_count = inputs.shape[0]
    lat_count = enc_weight.shape[2]
    all_rows = pairing.shape[0]
    n_lat = lax.psum(1, "latent")
    d_model = inputs.shape[2]
    chunk = d_model // n_lat
    partial_pre = jnp.einsum("rld,ldf->rf", inputs, enc_weight, preferred_element_type=jnp.float32)
    preact = lax.psum(partial_pre, "layer") + enc_bias
    features = jnp.maximum(preact, 0.0).astype(jnp.bfloat16)
    partial_recon = jnp.einsum(
        "rf,lfd->rld", features, dec_weight, preferred_element_type=jnp.float32
    )
    recon = (
        lax.psum(partial_recon.astype(jnp.bfloat16), "latent").astype(jnp.float32) + dec_bias[None]
    )
    recon_error = (recon - clean_acts.astype(jnp.float32)).astype(jnp.bfloat16)
    partial_grad = jnp.einsum(
        "rld,lfd->rf", recon_error, dec_weight, preferred_element_type=jnp.float32
    )
    feat_grad = lax.psum(partial_grad.astype(jnp.bfloat16), "layer").astype(jnp.float32)
    row_ids = lax.axis_index("row") * row_count + jnp.arange(row_count, dtype=jnp.int32)
    latent_ids = lax.axis_index("latent") * lat_count + jnp.arange(lat_count, dtype=jnp.int32)
    every_row = jnp.arange(all_rows, dtype=jnp.int32)
    pair_table = (
        (every_row[None, :] == row_ids[:, None]).astype(jnp.float32)
        - (pairing[None, :] == row_ids[:, None]).astype(jnp.float32)
    ).astype(jnp.bfloat16)
    target_hot = (targets[:, None] == latent_ids[None, :]).astype(jnp.bfloat16)
    margin_table = jnp.dot(pair_table, target_hot, preferred_element_type=jnp.float32)
    pre_grad = jnp.where(preact > 0, feat_grad - MARGIN * margin_table, 0.0).astype(jnp.bfloat16)
    enc_split = enc_weight[0].reshape(n_lat, chunk, lat_count)
    partial_input = jnp.einsum(
        "rf,gdf->grd", pre_grad, enc_split, preferred_element_type=jnp.float32
    ).astype(jnp.bfloat16)
    gathered = lax.all_to_all(partial_input, "latent", 0, 0, tiled=True)
    total = jnp.sum(gathered.astype(jnp.float32), axis=0).astype(jnp.bfloat16)
    return total[:, None, :]


def solution(mesh):
    placed = (
        P("row", "layer", None),
        P("row", "layer", None),
        P("layer", None, "latent"),
        P("latent"),
        P("layer", "latent", None),
        P("layer", None),
        P(),
        P(),
    )
    return jax.shard_map(
        local, mesh=mesh, in_specs=placed, out_specs=P("row", "layer", "latent"), check_vma=False
    )
```

profile of v0, /device:TPU:0, one launch (start us, length us, event | category | flops | bytes accessed | tf_op | source)
XLA Modules:
  0.0 292.9 jit_solution(8561482036106748665)
XLA Ops:
  6.5 0.0 copy-start.3
  6.5 0.0 all-reduce.4.cloned.1.call-start
  6.5 7.8 %fusion.3 = f32[512,768]{1,0:T(8,128)} fusion(bf16[1,3584,768]{2,1,0:T(8,128)(2,1)} %param.10, bf16[512,1,3584]{2,0,1:T(8,128)(2,1)} %param.8), kind=kOutput, calls=%fused_computation.5 | convolution fusion | flops 2818572288 | bytes 10747904 | tf_op jit(solution)/shard_map/rld,ldf->rf/dot_general | solution.py:16
  14.4 0.0 all-reduce.4.cloned.1.call-update
  14.4 0.0 all-reduce.6.cloned.1.call-start
  14.5 51.4 %all-reduce.4.cloned.1.call-done = f32[512,768]{1,0:T(8,128)} async-done(((f32[512,768]{1,0:T(8,128)}), f32[512,768]{1,0:T(8,128)}) %all-reduce.4.cloned.1.call-update) | async-done | bytes 1572880 | tf_op jit(solution)/shard_map/psum | solution.py:17
  65.8 0.0 copy-done.3
  65.8 7.9 %fusion.5 = bf16[512,1,3584]{2,0,1:T(8,128)(2,1)} fusion(bf16[1,768,3584]{2,1,0:T(8,128)(2,1)} %param.12, f32[512,768]{1,0:T(8,128)} %all-reduce.4.cloned.1.call-done, f32[768]{0:T(1024)S(1)} %copy-done.3), kind=kOutput, calls=%fused_computation.7 | convolution fusion | flops 2821586944 | bytes 10750976 | tf_op jit(solution)/shard_map/rf,lfd->rld/dot_general | solution.py:19
  73.7 0.0 copy-start
  73.7 0.0 all-reduce.6.cloned.1.call-update
  73.8 0.0 all-reduce.8.cloned.1.call-start
  73.8 0.6 copy-done
  74.5 0.0 copy-start.1
  74.5 0.0 copy-start.2
  74.5 0.0 copy-start.4
  74.5 99.5 %all-reduce.6.cloned.1.call-done = bf16[512,1,3584]{2,0,1:T(8,128)(2,1)} async-done(((bf16[512,1,3584]{2,0,1:T(8,128)(2,1)}), bf16[512,1,3584]{2,0,1:T(8,128)(2,1)}) %all-reduce.6.cloned.1.call-update) | async-done | bytes 3670032 | tf_op jit(solution)/shard_map/psum | solution.py:23
  174.0 8.8 %fusion.16 = bf16[512,768]{1,0:T(8,128)(2,1)} fusion(bf16[1,768,3584]{2,1,0:T(8,128)(2,1)} %param.12, bf16[512,1,3584]{2,0,1:T(8,128)(2,1)} %param.9, bf16[512,1,3584]{2,0,1:T(8,128)(2,1)} %all-reduce.6.cloned.1.call-done, f32[3584]{0:T(1024)S(1)} %reduce.1), kind=kOutput, calls=%fused_computation.20 | convolution fusion | flops 2828140544 | bytes 13645824 | tf_op jit(solution)/shard_map/rld,lfd->rf/dot_general | solution.py:26
  182.8 0.0 all-reduce.8.cloned.1.call-update
  182.8 38.6 %all-reduce.8.cloned.1.call-done = bf16[512,768]{1,0:T(8,128)(2,1)} async-done(((bf16[512,768]{1,0:T(8,128)(2,1)}), bf16[512,768]{1,0:T(8,128)(2,1)}) %all-reduce.8.cloned.1.call-update) | async-done | bytes 786448 | tf_op jit(solution)/shard_map/psum | solution.py:29
  221.4 0.0 copy-done.1
  221.4 0.0 copy-done.2
  221.5 0.0 copy-done.4
  221.5 8.9 %convert_bitcast_fusion = bf16[16,512,224]{1,2,0:T(8,128)(2,1)} fusion(bf16[16,224,768]{2,1,0:T(8,128)(2,1)} %bitcast.31, s32[768]{0:T(1024)S(1)} %iota_add_fusion, s32[1024]{0:T(1024)S(1)} %copy-done.2, bf16[512,768]{1,0:T(8,128)(2,1)} %all-reduce.8.cloned.1.call-done, f32[512,768]{1,0:T(8,128)S(1)} %copy-done.1, s32[1024]{0:T(1024)S(1)} %copy-done.4, ...), kind=kOutput, calls=%fused_computation.10 | convolution fusion | flops 3632398336 | bytes 11550720 | tf_op jit(solution)/shard_map/rf,gdf->grd/dot_general | solution.py:41
  230.4 52.8 %all_to_all.5 = bf16[16,512,224]{1,2,0:T(8,128)(2,1)} all-to-all(bf16[16,512,224]{1,2,0:T(8,128)(2,1)} %convert_bitcast_fusion), channel_id=1, replica_groups=mesh['layer'=4,'latent'=16,'row'=2] {'latent'}, dimensions={0} | all-to-all | bytes 7340032 | tf_op jit(solution)/shard_map/all_to_all | solution.py:44
  283.1 3.3 %reduce_sum.12 = bf16[512,224]{0,1:T(8,128)(2,1)} reduce(bf16[16,512,224]{1,2,0:T(8,128)(2,1)} %all_to_all.5, bf16[]{:T(256)} %constant.18.clone.1), dimensions={0}, to_apply=%region_3.4 | reduce | flops 1720320 | bytes 3899394 | tf_op jit(solution)/shard_map/reduce_sum | solution.py:45
  (3 shorter events, 0.0 us)
Async XLA Ops:
  6.5 59.3 %copy-start.3 = (f32[768]{0:T(1024)S(1)}, f32[768]{0:T(1024)}, u32[]{:S(2)}) copy-start(f32[768]{0:T(1024)} %param.11) | copy-start | bytes 9220
  6.5 59.3 %all-reduce.4.cloned.1.call-start = ((), (), s32[]{:S(2)}) async-start(), calls=%async_computation.1 | async-start | bytes 3145728 | tf_op jit(solution)/shard_map/psum | solution.py:17
  14.4 159.6 %all-reduce.6.cloned.1.call-start = ((), (), s32[]{:S(2)}) async-start(), calls=%async_computation.2 | async-start | bytes 7340032 | tf_op jit(solution)/shard_map/psum | solution.py:23
  73.7 0.7 copy-start
  73.8 147.7 %all-reduce.8.cloned.1.call-start = ((), (), s32[]{:S(2)}) async-start(), calls=%async_computation.3 | async-start | bytes 1572864 | tf_op jit(solution)/shard_map/psum | solution.py:29
  74.5 147.0 %copy-start.1 = (f32[512,768]{1,0:T(8,128)S(1)}, f32[512,768]{1,0:T(8,128)}, u32[]{:S(2)}) copy-start(f32[512,768]{1,0:T(8,128)} %all-reduce.4.cloned.1.call-done) | copy-start | bytes 4718596
  74.5 147.0 %copy-start.2 = (s32[1024]{0:T(1024)S(1)}, s32[1024]{0:T(1024)}, u32[]{:S(2)}) copy-start(s32[1024]{0:T(1024)} %param.15) | copy-start | bytes 12292
  74.5 146.9 %copy-start.4 = (s32[1024]{0:T(1024)S(1)}, s32[1024]{0:T(1024)}, u32[]{:S(2)}) copy-start(s32[1024]{0:T(1024)} %param.14) | copy-start | bytes 12292
Sparse Core Ops, SparseCore 0:
  14.5 51.2 all-reduce.3
  73.9 100.0 all-reduce.5
  182.9 38.4 all-reduce.7
where the time goes:
time: 293 us
  waiting for transfers between devices  190 us (65%)
  blocking collectives  52.8 us (18%)
  matrix products  33.4 us (11%)
  between operations  13.2 us (5%)
  other arithmetic  3.35 us (1%)
    psum x1, waiting for transfers between devices, local(): lax.psum(partial_recon.astype(jnp.bfloat16), 'latent').astype(jnp.float32)  99.5 us
    all_to_all x1, blocking collectives, local(): gathered = lax.all_to_all(partial_input, 'latent', 0, 0, tiled=True)  52.8 us
    psum x1, waiting for transfers between devices, local(): preact = lax.psum(partial_pre, 'layer') + enc_bias  51.4 us
    psum x1, waiting for transfers between devices, local(): lax.psum(partial_grad.astype(jnp.bfloat16), 'layer').astype(jnp.float32)  38.6 us
    dot_general x1, matrix products, local(): jnp.einsum('rf,gdf->grd', pre_grad, enc_split, preferred_element_type=jnp...  8.9 us
    dot_general x1, matrix products, local(): jnp.einsum('rld,lfd->rf', recon_error, dec_weight, preferred_element_type...  8.77 us
    dot_general x1, matrix products, local(): jnp.einsum('rf,lfd->rld', features, dec_weight, preferred_element_type=jn...  7.9 us
    dot_general x1, matrix products, local(): jnp.einsum('rld,ldf->rf', inputs, enc_weight, preferred_element_type=jnp....  7.84 us
  transfers between devices with their start and end apart: 3, of which 3 were waited for; matrix products, arithmetic and copies ran while one was open for 0% of the time, Pallas kernels for 0%

commit v1 on v0

--- a/solution.py
+++ b/solution.py
@@ -20,7 +20,10 @@
         "rf,lfd->rld", features, dec_weight, preferred_element_type=jnp.float32
     )
     recon = (
-        lax.psum(partial_recon.astype(jnp.bfloat16), "latent").astype(jnp.float32) + dec_bias[None]
+        jnp.sum(lax.all_gather(partial_recon.astype(jnp.bfloat16), "latent"), axis=0).astype(
+            jnp.float32
+        )
+        + dec_bias[None]
     )
     recon_error = (recon - clean_acts.astype(jnp.float32)).astype(jnp.bfloat16)
     partial_grad = jnp.einsum(

time: 293 us -> 542 us (1.85)
  waiting for transfers between devices: 190 us -> 417 us
  other arithmetic: 3.35 us -> 24.8 us
    all_gather x0 -> x1, waiting for transfers between devices: none -> 326 us  [local(): lax.all_gather(partial_recon.astype(jnp.bfloat16), 'latent')]
    psum x1 -> x0, waiting for transfers between devices: 99.5 us -> none  [local(): lax.psum(partial_recon.astype(jnp.bfloat16), 'latent').astype(jnp.float32)]
    reduce_sum x0 -> x1, other arithmetic: none -> 21.4 us  [local(): jnp.sum(lax.all_gather(partial_recon.astype(jnp.bfloat16), 'latent'), axi...]
where the time goes in v1:
time: 542 us
  waiting for transfers between devices  417 us (77%)
  blocking collectives  52.8 us (10%)
  matrix products  33.6 us (6%)
  other arithmetic  24.8 us (5%)
  between operations  13.1 us (2%)
    all_gather x1, waiting for transfers between devices, local(): lax.all_gather(partial_recon.astype(jnp.bfloat16), 'latent')  326 us
    all_to_all x1, blocking collectives, local(): gathered = lax.all_to_all(partial_input, 'latent', 0, 0, tiled=True)  52.8 us
    psum x1, waiting for transfers between devices, local(): preact = lax.psum(partial_pre, 'layer') + enc_bias  51.4 us
    psum x1, waiting for transfers between devices, local(): lax.psum(partial_grad.astype(jnp.bfloat16), 'layer').astype(jnp.float32)  39 us
    reduce_sum x1, other arithmetic, local(): jnp.sum(lax.all_gather(partial_recon.astype(jnp.bfloat16), 'latent'), axi...  21.4 us
  transfers between devices with their start and end apart: 3, of which 3 were waited for; matrix products, arithmetic and copies ran while one was open for 0% of the time, Pallas kernels for 0%

profile of v1, /device:TPU:0, one launch (start us, length us, event | category | flops | bytes accessed | tf_op | source)
XLA Modules:
  0.0 541.6 jit_solution(6447144840372823598)
XLA Ops:
  6.5 0.0 copy-start.3
  6.5 0.0 all-reduce.3.cloned.1.call-start
  6.5 8.0 %fusion.5 = f32[512,768]{1,0:T(8,128)} fusion(bf16[1,3584,768]{2,1,0:T(8,128)(2,1)} %param.10, bf16[512,1,3584]{2,0,1:T(8,128)(2,1)} %param.8), kind=kOutput, calls=%fused_computation.7 | convolution fusion | flops 2818572288 | bytes 10747904 | tf_op jit(solution)/shard_map/rld,ldf->rf/dot_general | solution.py:16
  14.5 0.0 all-reduce.3.cloned.1.call-update
  14.5 0.0 all-gather.3.cloned.1.call-start
  14.6 51.4 %all-reduce.3.cloned.1.call-done = f32[512,768]{1,0:T(8,128)} async-done(((f32[512,768]{1,0:T(8,128)}), f32[512,768]{1,0:T(8,128)}) %all-reduce.3.cloned.1.call-update) | async-done | bytes 1572880 | tf_op jit(solution)/shard_map/psum | solution.py:17
  65.9 0.0 copy-done.3
  65.9 7.9 %convolution_convert_fusion = bf16[512,3584]{1,0:T(8,128)(2,1)} fusion(bf16[1,768,3584]{2,1,0:T(8,128)(2,1)} %param.12, f32[512,768]{1,0:T(8,128)} %all-reduce.3.cloned.1.call-done, f32[768]{0:T(1024)S(1)} %copy-done.3), kind=kOutput, calls=%fused_computation.3 | convolution fusion | flops 2821586944 | bytes 10750976 | tf_op jit(solution)/shard_map/rf,lfd->rld/dot_general | solution.py:19
  73.8 0.0 copy-start
  73.8 0.0 all-gather.3.cloned.1.call-update
  73.8 0.2 all-reduce.5.cloned.1.call-start
  74.1 0.5 copy-done
  74.5 326.3 %all-gather.3.cloned.1.call-done = bf16[8192,3584]{1,0:T(8,128)(2,1)} async-done(((bf16[512,3584]{1,0:T(8,128)(2,1)}), bf16[8192,3584]{1,0:T(8,128)(2,1)}) %all-gather.3.cloned.1.call-update) | async-done | bytes 58720272 | tf_op jit(solution)/shard_map/all_gather | solution.py:23
  400.8 21.4 %reduce.3 = bf16[512,3584]{1,0:T(8,128)(2,1)} reduce(bf16[16,512,3584]{2,1,0:T(8,128)(2,1)} %bitcast.36, bf16[]{:T(256)} %constant.5.clone.1), dimensions={0}, to_apply=%region_1.0 | reduce | flops 27525120 | bytes 62390272 | tf_op jit(solution)/shard_map/reduce_sum | solution.py:23
  422.2 0.0 copy-start.1
  422.2 0.0 copy-start.2
  422.2 0.0 copy-start.4
  422.2 8.9 %fusion.16 = bf16[512,768]{1,0:T(8,128)(2,1)} fusion(bf16[1,768,3584]{2,1,0:T(8,128)(2,1)} %param.12, bf16[512,1,3584]{2,0,1:T(8,128)(2,1)} %param.9, bf16[512,3584]{1,0:T(8,128)(2,1)} %reduce.3, f32[3584]{0:T(1024)S(1)} %reduce.4), kind=kOutput, calls=%fused_computation.22 | convolution fusion | flops 2828140544 | bytes 13645824 | tf_op jit(solution)/shard_map/rld,lfd->rf/dot_general | solution.py:29
  431.1 0.0 all-reduce.5.cloned.1.call-update
  431.2 39.0 %all-reduce.5.cloned.1.call-done = bf16[512,768]{1,0:T(8,128)(2,1)} async-done(((bf16[512,768]{1,0:T(8,128)(2,1)}), bf16[512,768]{1,0:T(8,128)(2,1)}) %all-reduce.5.cloned.1.call-update) | async-done | bytes 786448 | tf_op jit(solution)/shard_map/psum | solution.py:32
  470.1 0.0 copy-done.1
  470.1 0.0 copy-done.2
  470.2 0.0 copy-done.4
  470.2 8.9 %convert_bitcast_fusion = bf16[16,512,224]{1,2,0:T(8,128)(2,1)} fusion(bf16[16,224,768]{2,1,0:T(8,128)(2,1)} %bitcast.37, s32[768]{0:T(1024)S(1)} %iota_add_fusion, s32[1024]{0:T(1024)S(1)} %copy-done.2, bf16[512,768]{1,0:T(8,128)(2,1)} %all-reduce.5.cloned.1.call-done, f32[512,768]{1,0:T(8,128)S(1)} %copy-done.1, s32[1024]{0:T(1024)S(1)} %copy-done.4, ...), kind=kOutput, calls=%fused_computation.12 | convolution fusion | flops 3632398336 | bytes 11550720 | tf_op jit(solution)/shard_map/rf,gdf->grd/dot_general | solution.py:44
  479.1 52.8 %all_to_all.5 = bf16[16,512,224]{1,2,0:T(8,128)(2,1)} all-to-all(bf16[16,512,224]{1,2,0:T(8,128)(2,1)} %convert_bitcast_fusion), channel_id=1, replica_groups=mesh['layer'=4,'latent'=16,'row'=2] {'latent'}, dimensions={0} | all-to-all | bytes 7340032 | tf_op jit(solution)/shard_map/all_to_all | solution.py:47
  531.8 3.3 reduce_sum.25
  (3 shorter events, 0.0 us)
Async XLA Ops:
  6.5 59.4 %copy-start.3 = (f32[768]{0:T(1024)S(1)}, f32[768]{0:T(1024)}, u32[]{:S(2)}) copy-start(f32[768]{0:T(1024)} %param.11) | copy-start | bytes 9220
  6.5 59.4 %all-reduce.3.cloned.1.call-start = ((), (), s32[]{:S(2)}) async-start(), calls=%async_computation.1 | async-start | bytes 3145728 | tf_op jit(solution)/shard_map/psum | solution.py:17
  14.5 386.3 %all-gather.3.cloned.1.call-start = ((), (), s32[]{:S(2)}) async-start(), calls=%async_computation.3 | async-start | bytes 62390272 | tf_op jit(solution)/shard_map/all_gather | solution.py:23
  73.8 0.7 copy-start
  73.8 396.3 %all-reduce.5.cloned.1.call-start = ((), (), s32[]{:S(2)}) async-start(), calls=%async_computation.2 | async-start | bytes 1572864 | tf_op jit(solution)/shard_map/psum | solution.py:32
  422.2 47.9 %copy-start.1 = (f32[512,768]{1,0:T(8,128)S(1)}, f32[512,768]{1,0:T(8,128)}, u32[]{:S(2)}) copy-start(f32[512,768]{1,0:T(8,128)} %all-reduce.3.cloned.1.call-done) | copy-start | bytes 4718596
  422.2 47.9 %copy-start.2 = (s32[1024]{0:T(1024)S(1)}, s32[1024]{0:T(1024)}, u32[]{:S(2)}) copy-start(s32[1024]{0:T(1024)} %param.15) | copy-start | bytes 12292
  422.2 47.9 %copy-start.4 = (s32[1024]{0:T(1024)S(1)}, s32[1024]{0:T(1024)}, u32[]{:S(2)}) copy-start(s32[1024]{0:T(1024)} %param.14) | copy-start | bytes 12292
Sparse Core Ops, SparseCore 0:
  14.6 51.2 all-reduce.2
  73.9 326.8 all-gather.2
  431.2 38.8 all-reduce.4
